TPU v7x, 32 devices: a whole 2x2x4 slice. The times are simulated.
32 devices in a mesh: ex: 8 (over z, y), tp: 4 (over x, core).
Axes of the slice: x: 2, y: 2, z: 4, core: 2. Of those that a mesh axis runs over, the one named last changes fastest.
Arguments:
- residual_in: bfloat16 [1536, 2880], P('ex', 'tp'), may hold values from -40 to 40
- queries: bfloat16 [1536, 2048], P('ex', 'tp'), may hold values from -4 to 4
- keys_values: bfloat16 [1536, 4, 128], P('ex', 'tp'), may hold values from -4 to 4
- sink_logits: float32 [32], P('tp'), may hold values from 1 to 6
- out_proj: bfloat16 [2048, 2880], P('tp'), may hold values from -0.75 to 0.75
- norm_gain: float32 [2880], replicated, may hold values from 0.25 to 1.75
- routes: int32 [1536, 4], P('ex'), may hold values from 0 to 7, all different within a row; in each aligned block of 192 rows (0 to 191, 192 to 383, ...) at most 160 rows name the same one
- route_scores: int32 [1536, 4], P('ex'), may hold values from 1 to 8
- tenants: int32 [1536], P('ex'), may hold values from 0 to 7
- gate_up: bfloat16 [8, 2880, 2, 1536], P('ex', None, None, 'tp'), may hold values from -0.109375 to 0.109375
- adapter_in: bfloat16 [8, 2880, 128], P('ex'), may hold values from -0.109375 to 0.109375
- adapter_out: bfloat16 [8, 128, 2, 1536], P('ex', None, None, 'tp'), may hold values from -1.5 to 1.5
- down_proj: bfloat16 [8, 1536, 2880], P('ex', 'tp'), may hold values from -0.15625 to 0.15625
Outputs:
- residual_out: bfloat16 [1536, 2880], P('ex', 'tp')
- expert_mix: bfloat16 [1536, 2880], P('ex', 'tp')
Inputs may be any that keep to these rules, and one draw needn't show every extreme that they name: `routes`: among the 192 rows of one device (aligned blocks), no expert is named by more than 160 rows, and in every draw some expert is named by exactly 160 rows of some block.
All inputs are finite; a program needn't handle non-finite values.
Results may differ from a plain program's by a relative error of at most 0.023.
Values may be sent and summed in bfloat16 or wider, within the bound.
A program may use at most 128 MiB of HBM per device.

v0:
```python
import jax
import jax.numpy as jnp
from jax import lax
from jax.sharding import PartitionSpec as P

WINDOW = 128
TOP = 4
RANK = 16


def from_behind(value, axis, steps):
    count = lax.axis_size(axis)
    initial, last = (max(0, -steps), min(count, count - steps))
    return lax.ppermute(value, axis, [(source, source + steps) for source in range(initial, last)])


def shards(
    residual_in,
    queries,
    keys_values,
    sink_logits,
    out_proj,
    norm_gain,
    routes,
    route_scores,
    tenants,
    gate_up,
    adapter_in,
    adapter_out,
    down_proj,
):
    tok_rows = residual_in.shape[0]
    columns = residual_in.shape[1]
    width = out_proj.shape[1]
    heads_here = sink_logits.shape[0]
    kv_here = keys_values.shape[1]
    group_size = heads_here // kv_here
    head_size = keys_values.shape[2] // 2
    rim_rows = WINDOW - 1
    table = token_table(routes, route_scores, tenants, gate_up.shape[0] * lax.axis_size("ex"))
    before = from_behind(keys_values[tok_rows - rim_rows :], "ex", 1)
    extended = jnp.concatenate([before, keys_values], axis=0)
    keys_only = extended[:, :, :head_size]
    values_only = extended[:, :, head_size:]
    query_rows = queries.reshape(tok_rows, kv_here, group_size, head_size)
    scores = jnp.einsum(
        "tcgd,jcd->cgtj", query_rows, keys_only, preferred_element_type=jnp.float32
    ) * head_size ** (-0.5)
    start = lax.axis_index("ex") * tok_rows
    query_pos = start + jnp.arange(tok_rows, dtype=jnp.int32)
    key_pos = start - rim_rows + jnp.arange(tok_rows + rim_rows, dtype=jnp.int32)
    distance = query_pos[:, None] - key_pos[None, :]
    allowed = (distance >= 0) & (distance < WINDOW) & (key_pos[None, :] >= 0)
    numerators = jnp.where(allowed, jnp.exp(scores), 0.0)
    totals = jnp.exp(sink_logits.reshape(kv_here, group_size))[:, :, None] + jnp.sum(
        numerators, axis=-1
    )
    weights = (numerators / totals[..., None]).astype(jnp.bfloat16)
    attended = jnp.einsum(
        "cgtj,jcd->tcgd", weights, values_only, preferred_element_type=jnp.float32
    )
    attended = attended.astype(jnp.bfloat16).reshape(tok_rows, heads_here * head_size)
    head_terms = jnp.dot(attended, out_proj, preferred_element_type=jnp.float32)
    head_share = lax.psum_scatter(
        head_terms.astype(jnp.bfloat16), "tp", scatter_dimension=1, tiled=True
    ).astype(jnp.float32)
    residual_out = (residual_in.astype(jnp.float32) + head_share).astype(jnp.bfloat16)
    sources = lax.axis_size("ex")
    experts_all = gate_up.shape[0] * sources
    capacity = 5 * tok_rows * TOP // (3 * experts_all)
    if gate_up.shape[0] == 1 and 2 * capacity >= tok_rows:
        mixed = dense_experts(
            residual_out, table, norm_gain, gate_up, adapter_in, adapter_out, down_proj
        )
        return (residual_out, mixed)
    return (
        residual_out,
        routed_experts(
            residual_out,
            norm_gain,
            routes,
            route_scores,
            tenants,
            gate_up,
            adapter_in,
            adapter_out,
            down_proj,
            columns,
        ),
    )


def token_table(routes, route_scores, tenants, experts_all):
    score_float = route_scores.astype(jnp.float32)
    share = score_float / jnp.sum(score_float, axis=1, keepdims=True)
    hit = routes[:, :, None] == jnp.arange(experts_all, dtype=jnp.int32)[None, None, :]
    by_expert = jnp.sum(jnp.where(hit, share[:, :, None], 0.0), axis=1)
    return jnp.concatenate([by_expert, tenants.astype(jnp.float32)[:, None]], axis=1)


def dense_experts(residual_out, table, norm_gain, gate_up, adapter_in, adapter_out, down_proj):
    tok_rows, columns = residual_out.shape
    sources = lax.axis_size("ex")
    quarters = lax.axis_size("tp")
    width = columns * quarters
    rows_all = sources * tok_rows
    hidden_here = gate_up.shape[3]
    rank_cols = adapter_in.shape[2]
    tokens = gather_tokens(residual_out)
    whole_rows = tokens.astype(jnp.float32)
    inverse = lax.rsqrt(jnp.mean(whole_rows * whole_rows, axis=-1, keepdims=True) + 1e-05)
    normed = (whole_rows * inverse * norm_gain).astype(jnp.bfloat16)
    everyone = lax.all_gather(table, "ex", axis=0, tiled=True)
    expert = lax.axis_index("ex")
    here = jnp.arange(everyone.shape[1], dtype=jnp.int32)[None, :] == expert
    weight = jnp.sum(jnp.where(here, everyone, 0.0), axis=1, keepdims=True)
    tenant = everyone[:, -1:].astype(jnp.int32)
    mapped = jnp.dot(
        normed, gate_up[0].reshape(width, 2 * hidden_here), preferred_element_type=jnp.float32
    )
    low_rank = jnp.dot(normed, adapter_in[0], preferred_element_type=jnp.float32)
    keep = (jnp.arange(rank_cols, dtype=jnp.int32) // RANK)[None, :] == tenant
    low_rank = jnp.where(keep, low_rank, 0.0).astype(jnp.bfloat16)
    mapped = mapped + jnp.dot(
        low_rank,
        adapter_out[0].reshape(rank_cols, 2 * hidden_here),
        preferred_element_type=jnp.float32,
    )
    gate_part = mapped[:, :hidden_here]
    up_part = mapped[:, hidden_here:]
    activated = (gate_part * jax.nn.sigmoid(1.702 * gate_part) * (up_part + 1.0) * weight).astype(
        jnp.bfloat16
    )
    terms = jnp.dot(activated, down_proj[0], preferred_element_type=jnp.float32).astype(
        jnp.bfloat16
    )
    return scatter_terms(terms)


def gather_tokens(residual_out):
    tok_rows, columns = residual_out.shape
    sources, quarters = (lax.axis_size("ex"), lax.axis_size("tp"))
    blocks = lax.all_gather(residual_out, ("ex", "tp"), axis=0, tiled=False)
    blocks = blocks.reshape(sources, quarters, tok_rows, columns).transpose(0, 2, 1, 3)
    return blocks.reshape(sources * tok_rows, quarters * columns)


def scatter_terms(terms):
    mine = lax.psum_scatter(terms, "tp", scatter_dimension=1, tiled=True)
    return lax.psum_scatter(mine, "ex", scatter_dimension=0, tiled=True)


def routed_experts(
    residual_out,
    norm_gain,
    routes,
    route_scores,
    tenants,
    gate_up,
    adapter_in,
    adapter_out,
    down_proj,
    columns,
):
    tok_rows = residual_out.shape[0]
    width = gate_up.shape[1]
    whole_rows = lax.all_gather(residual_out, "tp", axis=1, tiled=True).astype(jnp.float32)
    inverse = lax.rsqrt(jnp.mean(whole_rows * whole_rows, axis=-1, keepdims=True) + 1e-05)
    normed = (whole_rows * inverse * norm_gain).astype(jnp.bfloat16)
    sources = lax.axis_size("ex")
    local_count = gate_up.shape[0]
    experts_all = local_count * sources
    capacity = 5 * tok_rows * TOP // (3 * experts_all)
    pair_count = tok_rows * TOP
    route_flat = routes.reshape(pair_count)
    one_hot = (route_flat[:, None] == jnp.arange(experts_all, dtype=jnp.int32)[None, :]).astype(
        jnp.int32
    )
    earlier = jnp.cumsum(one_hot, axis=0) - one_hot
    slot = jnp.sum(earlier * one_hot, axis=1)
    target = route_flat * capacity + slot
    pair_of = (
        jnp.full((experts_all * capacity,), pair_count, jnp.int32)
        .at[target]
        .set(jnp.arange(pair_count, dtype=jnp.int32))
    )
    token_of = pair_of // TOP
    send_width = normed.shape[1]
    normed_pad = jnp.concatenate([normed, jnp.zeros((1, send_width), jnp.bfloat16)], axis=0)
    tenant_pad = jnp.concatenate([tenants, jnp.zeros((1,), jnp.int32)])
    sent_rows = normed_pad[token_of].reshape(experts_all, capacity, send_width)
    sent_tenants = tenant_pad[token_of].reshape(experts_all, capacity)
    received, got_tenants = (
        lax.all_to_all(sent_rows, "ex", split_axis=0, concat_axis=0, tiled=True),
        lax.all_to_all(sent_tenants, "ex", split_axis=0, concat_axis=0, tiled=True),
    )
    hidden_here = gate_up.shape[3]
    rank_cols = adapter_in.shape[2]
    arrived = received.reshape(sources, local_count, capacity, width)
    arrived_tenants = got_tenants.reshape(sources, local_count, capacity)
    slot_rows = arrived[:, 0].reshape(sources * capacity, width)
    slot_tenant = arrived_tenants[:, 0].reshape(sources * capacity)
    mapped = jnp.dot(
        slot_rows, gate_up[0].reshape(width, 2 * hidden_here), preferred_element_type=jnp.float32
    )
    low_rank = jnp.dot(slot_rows, adapter_in[0], preferred_element_type=jnp.float32)
    keep = (jnp.arange(rank_cols, dtype=jnp.int32) // RANK)[None, :] == slot_tenant[:, None]
    low_rank = jnp.where(keep, low_rank, 0.0).astype(jnp.bfloat16)
    mapped = mapped + jnp.dot(
        low_rank,
        adapter_out[0].reshape(rank_cols, 2 * hidden_here),
        preferred_element_type=jnp.float32,
    )
    gate_part = mapped[:, :hidden_here]
    up_part = mapped[:, hidden_here:]
    activated = (gate_part * jax.nn.sigmoid(1.702 * gate_part) * (up_part + 1.0)).astype(
        jnp.bfloat16
    )
    quarter = jnp.dot(activated, down_proj[0], preferred_element_type=jnp.float32).astype(
        jnp.bfloat16
    )
    outputs = quarter.reshape(sources, 1, capacity, width)
    quarters = outputs.reshape(sources * local_count, capacity, width)
    score_float = route_scores.astype(jnp.float32)
    route_weight = (score_float / jnp.sum(score_float, axis=1, keepdims=True)).reshape(pair_count)
    shares = lax.psum_scatter(
        quarters.astype(jnp.float32).astype(jnp.bfloat16), "tp", scatter_dimension=2, tiled=True
    ).astype(jnp.float32)
    returned = lax.all_to_all(
        shares.astype(jnp.bfloat16), "ex", split_axis=0, concat_axis=0, tiled=True
    ).astype(shares.dtype)
    picked = returned.reshape(experts_all * capacity, columns)[target]
    expert_mix = jnp.sum((picked * route_weight[:, None]).reshape(tok_rows, TOP, columns), axis=1)
    return expert_mix.astype(jnp.bfloat16)


def solution(mesh):
    in_specs = (
        P("ex", "tp"),
        P("ex", "tp"),
        P("ex", "tp", None),
        P("tp"),
        P("tp", None),
        P(),
        P("ex", None),
        P("ex", None),
        P("ex"),
        P("ex", None, None, "tp"),
        P("ex", None, None),
        P("ex", None, None, "tp"),
        P("ex", "tp", None),
    )
    out_specs = (P("ex", "tp"), P("ex", "tp"))
    return jax.shard_map(shards, mesh=mesh, in_specs=in_specs, out_specs=out_specs, check_vma=False)
```

profile of v0, /device:TPU:0, one launch (start us, length us, event | category | flops | bytes accessed | tf_op | source)
XLA Modules:
  0.0 385.4 jit_solution(12304677267419445353)
XLA Ops:
  7.2 1.0 copy.43
  8.3 0.1 slice.24
  8.4 4.9 %collective-permute-start = (bf16[127,1,128]{0,2,1:T(8,128)(2,1)S(1)}, bf16[127,1,128]{0,2,1:T(8,128)(2,1)S(1)}, u32[]{:S(2)}, u32[]{:S(2)}) collective-permute-start(bf16[127,1,128]{0,2,1:T(8,128)(2,1)S(1)} %slice.24), channel_id=1, source_target_pairs={{0,4},{4,8},{8,12},{12,16},{16,20},{20,24},{24,28},{1,5},{5,9},{9,... | collective-permute-start | bytes 97544 | tf_op jit(solution)/shard_map/ppermute | solution.py:14
  13.3 0.1 fusion.21
  13.5 1.1 copy.45
  14.5 0.7 exp.19
  15.2 0.9 fusion.8
  16.1 0.1 broadcast_add_fusion
  16.2 0.8 convolution_convert_fusion.2
  17.0 2.1 convolution_convert_fusion.1
  19.2 2.5 copy.49
  21.7 0.0 all-gather.4.cloned.1.call-start
  21.8 29.2 %reduce-scatter.10.cloned.1.call-done = bf16[720,192]{1,0:T(8,128)(2,1)} async-done(((bf16[2880,192]{1,0:T(8,128)(2,1)}), bf16[720,192]{1,0:T(8,128)(2,1)}) %reduce-scatter.10.cloned.1.call-update) | async-done | bytes 276496
  51.0 1.1 copy.50
  52.1 0.8 add_convert_fusion
  52.9 0.0 reduce-scatter.8.cloned.1.call-start
  53.0 0.1 mul.66
  53.1 5.2 %copy.53 = bf16[360,8,2,384]{3,1,2,0:T(8,128)(2,1)} copy(bf16[360,8,2,384]{3,2,1,0:T(2,128)(2,1)} %bitcast.65) | data formatting | bytes 8847360
  58.4 31.1 %all-gather.1 = f32[8,192,9]{1,2,0:T(8,128)S(1)} all-gather(f32[1,192,9]{1,2,0:T(8,128)S(1)} %maximum_bitcast_fusion), channel_id=1, replica_groups=mesh['ex'=8,'tp'=4] {'ex'}, dimensions={0}, use_global_device_ids=true | all-gather | bytes 62208 | tf_op jit(solution)/shard_map/all_gather | solution.py:113
  89.5 0.1 reshape.136
  89.7 0.1 select_reduce_fusion
  89.8 46.3 %all-gather.4.cloned.1.call-done = bf16[6144,720]{1,0:T(8,128)(2,1)} async-done(((bf16[192,720]{1,0:T(8,128)(2,1)}), bf16[6144,720]{1,0:T(8,128)(2,1)}) %all-gather.4.cloned.1.call-update) | async-done | bytes 8847376 | tf_op jit(solution)/shard_map/all_gather | solution.py:143
  136.1 12.6 %convert.1 = f32[8,4,192,720]{3,2,1,0:T(8,128)} convert(bf16[8,4,192,720]{3,2,1,0:T(8,128)(2,1)} %bitcast.62) | non-fusion elementwise | flops 4423680 | bytes 26542080 | tf_op jit(solution)/shard_map/convert_element_type | solution.py:110
  148.7 5.8 %multiply_reduce_fusion = f32[8,192]{1,0:T(8,128)S(1)} fusion(bf16[8,4,192,720]{3,2,1,0:T(8,128)(2,1)} %bitcast.63), kind=kLoop, calls=%fused_computation.3 | loop fusion | flops 13269504 | bytes 8853504 | tf_op jit(solution)/shard_map/reduce_sum | solution.py:111
  154.5 23.8 %fusion.2 = bf16[8,192,4,720]{3,2,1,0:T(4,128)(2,1)} fusion(f32[8,4,192,720]{3,2,1,0:T(8,128)} %convert.1, f32[4,720]{1,0:T(4,128)S(1)} %mul.66, f32[8,192]{1,0:T(8,128)S(1)} %add_rsqrt_fusion), kind=kLoop, calls=%fused_computation.5 | loop fusion | flops 13271040 | bytes 26559744 | tf_op jit(solution)/shard_map/convert_element_type | solution.py:112
  178.3 17.7 %convert_element_type.74 = bf16[1536,2880]{1,0:T(8,128)(2,1)} reshape(bf16[8,192,4,720]{3,2,1,0:T(4,128)(2,1)} %fusion.2) | data formatting | bytes 17694720 | tf_op jit(solution)/shard_map/convert_element_type | solution.py:112
  196.1 12.8 %fusion.37 = f32[1536,768]{1,0:T(8,128)} fusion(bf16[1536,2880]{1,0:T(8,128)(2,1)} %convert_element_type.74, bf16[2880,768]{1,0:T(8,128)(2,1)} %bitcast.66), kind=kOutput, calls=%fused_computation.66 | convolution fusion | flops 6794772480 | bytes 17989632 | tf_op jit(solution)/shard_map/dot_general | solution.py:118
  208.9 11.2 %convolution_add_fusion = f32[1536,768]{1,0:T(8,128)} fusion(f32[1536,768]{1,0:T(8,128)} %fusion.37, bf16[128,768]{1,0:T(8,128)(2,1)S(1)} %bitcast.67, bf16[1536,2880]{1,0:T(8,128)(2,1)} %convert_element_type.74, bf16[1,2880,128]{2,1,0:T(8,128)(2,1)S(1)} %copy-done.2, s32[128]{0:T(128)S(1)} %and_select_fusion, s32[1536]{0:T(1024)S(1)} %fusion.29), kind=kOutput, calls=%fused_computation.6 | convolution fusion | flops 1436221440 | bytes 19225088 | tf_op jit(solution)/shard_map/dot_general | solution.py:124
  220.1 11.5 %convolution_convert_fusion = bf16[1536,2880]{0,1:T(8,128)(2,1)} fusion(bf16[1,384,2880]{1,2,0:T(8,128)(2,1)} %param.25, f32[1536,768]{1,0:T(8,128)} %convolution_add_fusion, f32[1536]{0:T(1024)S(1)} %select_reduce_fusion), kind=kOutput, calls=%fused_computation.4 | convolution fusion | flops 3407118336 | bytes 15783936 | tf_op jit(solution)/shard_map/dot_general | solution.py:134
  231.6 72.8 %reduce-scatter.8.cloned.1.call-done = bf16[1536,720]{0,1:T(8,128)(2,1)} async-done(((bf16[1536,2880]{0,1:T(8,128)(2,1)}), bf16[1536,720]{0,1:T(8,128)(2,1)}) %reduce-scatter.8.cloned.1.call-update) | async-done | bytes 2211856 | tf_op jit(solution)/shard_map/reduce_scatter | solution.py:149
  304.5 4.2 %copy.51 = bf16[1536,720]{1,0:T(8,128)(2,1)} copy(bf16[1536,720]{0,1:T(8,128)(2,1)} %reduce-scatter.8.cloned.1.call-done) | data formatting | bytes 4423680
  308.7 70.1 %reduce-scatter.12.cloned.1.call-done = bf16[192,720]{1,0:T(8,128)(2,1)} async-done(((bf16[1536,720]{1,0:T(8,128)(2,1)}), bf16[192,720]{1,0:T(8,128)(2,1)}) %reduce-scatter.12.cloned.1.call-update) | async-done | bytes 276496
  (39 shorter events, 0.4 us)
Async XLA Ops:
  7.2 9.9 %copy-start = (bf16[512,2880]{0,1:T(8,128)(2,1)S(1)}, bf16[512,2880]{0,1:T(8,128)(2,1)}, u32[]{:S(2)}) copy-start(bf16[512,2880]{0,1:T(8,128)(2,1)} %param.17) | copy-start | bytes 8847364
  7.2 43.8 %reduce-scatter.10.cloned.1.call-start = ((), (), s32[]{:S(2)}) async-start(), calls=%async_computation.5 | async-start | bytes 1843200
  8.4 6.8 %collective-permute-start = (bf16[127,1,128]{0,2,1:T(8,128)(2,1)S(1)}, bf16[127,1,128]{0,2,1:T(8,128)(2,1)S(1)}, u32[]{:S(2)}, u32[]{:S(2)}) collective-permute-start(bf16[127,1,128]{0,2,1:T(8,128)(2,1)S(1)} %slice.24), channel_id=1, source_target_pairs={{0,4},{4,8},{8,12},{12,16},{16,20},{20,24},{24,28},{1,5},{5,9},{9,... | collective-permute-start | bytes 97544 | tf_op jit(solution)/shard_map/ppermute | solution.py:14
  19.1 33.0 %copy-start.3 = (bf16[192,720]{1,0:T(8,128)(2,1)S(1)}, bf16[192,720]{1,0:T(8,128)(2,1)}, u32[]{:S(2)}) copy-start(bf16[192,720]{1,0:T(8,128)(2,1)} %param.13) | copy-start | bytes 829444
  19.2 33.8 %copy-start.6 = (f32[2880]{0:T(1024)S(1)}, f32[2880]{0:T(1024)}, u32[]{:S(2)}) copy-start(f32[2880]{0:T(1024)} %param.18) | copy-start | bytes 34564
  21.7 114.4 %all-gather.4.cloned.1.call-start = ((), (), s32[]{:S(2)}) async-start(), calls=%async_computation.4 | async-start | bytes 9732096 | tf_op jit(solution)/shard_map/all_gather | solution.py:143
  52.9 251.6 %reduce-scatter.8.cloned.1.call-start = ((), (), s32[]{:S(2)}) async-start(), calls=%async_computation.3 | async-start | bytes 11059200 | tf_op jit(solution)/shard_map/reduce_scatter | solution.py:149
  53.1 5.2 %copy-start.8 = (s32[192]{0:T(256)S(1)}, s32[192]{0:T(256)}, u32[]{:S(2)}) copy-start(s32[192]{0:T(256)} %param.21) | copy-start | bytes 2308
  53.1 5.2 %copy-start.5 = (s32[192,4]{0,1:T(4,128)S(1)}, s32[192,4]{0,1:T(4,128)}, u32[]{:S(2)}) copy-start(s32[192,4]{0,1:T(4,128)} %param.20) | copy-start | bytes 9220
  53.1 5.2 %copy-start.7 = (s32[192,4]{0,1:T(4,128)S(1)}, s32[192,4]{0,1:T(4,128)}, u32[]{:S(2)}) copy-start(s32[192,4]{0,1:T(4,128)} %param.19) | copy-start | bytes 9220
  53.1 36.5 %copy-start.4 = (bf16[1,128,2,384]{3,2,1,0:T(2,128)(2,1)S(1)}, bf16[1,128,2,384]{3,2,1,0:T(2,128)(2,1)}, u32[]{:S(2)}) copy-start(bf16[1,128,2,384]{3,2,1,0:T(2,128)(2,1)} %param.24) | copy-start | bytes 589828
  196.1 12.8 %copy-start.2 = (bf16[1,2880,128]{2,1,0:T(8,128)(2,1)S(1)}, bf16[1,2880,128]{2,1,0:T(8,128)(2,1)}, u32[]{:S(2)}) copy-start(bf16[1,2880,128]{2,1,0:T(8,128)(2,1)} %param.23) | copy-start | bytes 2211844
  231.6 147.2 %copy-start.1 = (bf16[512,2880]{0,1:T(8,128)(2,1)S(1)}, bf16[512,2880]{0,1:T(8,128)(2,1)}, u32[]{:S(2)}) copy-start(bf16[512,2880]{0,1:T(8,128)(2,1)} %param.17) | copy-start | bytes 8847364
  231.6 147.2 %reduce-scatter.12.cloned.1.call-start = ((), (), s32[]{:S(2)}) async-start(), calls=%async_computation.6 | async-start | bytes 2654208
Sparse Core Ops, SparseCore 0:
  21.8 29.1 reduce-scatter.9
  54.4 81.6 all-gather.3
  231.7 72.7 reduce-scatter.7
  308.9 69.9 reduce-scatter.11
where the time goes:
time: 386 us; the launch traced here: 385 us
  waiting for transfers between devices  219 us (57%)
  other arithmetic  43.4 us (11%)
  matrix products  39.4 us (10%)
  local copies, waits for them, and re-layouts  33.9 us (9%)
  blocking collectives  31.1 us (8%)
  between operations  14 us (4%)
  starting transfers between devices  5.06 us (1%)
    unnamed x6, waiting for transfers between devices  99.4 us
    reduce_scatter x1, waiting for transfers between devices, scatter_terms(): mine = lax.psum_scatter(terms, 'tp', scatter_dimension=1, tiled=True)  72.8 us
    all_gather x1, waiting for transfers between devices, gather_tokens(): blocks = lax.all_gather(residual_out, ('ex', 'tp'), axis=0, tiled=False)  46.3 us
    all_gather x1, blocking collectives, dense_experts(): everyone = lax.all_gather(table, 'ex', axis=0, tiled=True)  31.1 us
    convert_element_type x1, other arithmetic, dense_experts(): normed = (whole_rows * inverse * norm_gain).astype(jnp.bfloat16)  23.8 us
    convert_element_type x1, local copies, waits for them, and re-layouts, dense_experts(): normed = (whole_rows * inverse * norm_gain).astype(jnp.bfloat16)  17.7 us
    unnamed x26, local copies, waits for them, and re-layouts  15.3 us
    dot_general x1, matrix products, dense_experts(): jnp.dot(normed, gate_up[0].reshape(width, 2 * hidden_here), preferred_ele...  12.8 us
  transfers between devices with their start and end apart: 5, of which 4 were waited for; matrix products, arithmetic and copies ran while one was open for 2% of the time, Pallas kernels for 0%

commit v1 on v0

--- a/solution.py
+++ b/solution.py
@@ -110,7 +110,12 @@
     whole_rows = tokens.astype(jnp.float32)
     inverse = lax.rsqrt(jnp.mean(whole_rows * whole_rows, axis=-1, keepdims=True) + 1e-05)
     normed = (whole_rows * inverse * norm_gain).astype(jnp.bfloat16)
-    everyone = lax.all_gather(table, "ex", axis=0, tiled=True)
+    ring = [table]
+    for hop in range(7):
+        ring.append(lax.ppermute(ring[-1], "ex", [(dev, (dev + 1) % 8) for dev in range(8)]))
+    everyone = jnp.roll(
+        jnp.concatenate(ring[::-1], axis=0), (lax.axis_index("ex") + 1) * ring[0].shape[0], axis=0
+    )
     expert = lax.axis_index("ex")
     here = jnp.arange(everyone.shape[1], dtype=jnp.int32)[None, :] == expert
     weight = jnp.sum(jnp.where(here, everyone, 0.0), axis=1, keepdims=True)

time: 386 us -> 386 us (level)
  blocking collectives: 31.1 us -> 0 us
  waiting for transfers between devices: 219 us -> 248 us
    ppermute x0 -> x7, waiting for transfers between devices: none -> 39.2 us  [dense_experts(): lax.ppermute(ring[-1], 'ex', [(dev, (dev + 1) % 8) for dev in range(8)])]
    all_gather x1 -> x0, blocking collectives: 31.1 us -> none  [dense_experts(): everyone = lax.all_gather(table, 'ex', axis=0, tiled=True)]
    all_gather x1, waiting for transfers between devices: 46.3 us -> 36.7 us  [gather_tokens(): blocks = lax.all_gather(residual_out, ('ex', 'tp'), axis=0, tiled=False)]
    unnamed x26 -> x25, local copies, waits for them, and re-layouts: 15.3 us -> 15.3 us
  transfers between devices with their start and end apart: 5 -> 12, of which waited for: 4 -> 11; matrix products, arithmetic and copies ran while one was open for 2% -> 2% of each run, Pallas kernels for 0% -> 0%
where the time goes in v1:
time: 386 us; the launch traced here: 385 us
  waiting for transfers between devices  248 us (64%)
  other arithmetic  43.4 us (11%)
  matrix products  39.4 us (10%)
  local copies, waits for them, and re-layouts  33.9 us (9%)
  between operations  14 us (4%)
  starting transfers between devices  6.59 us (2%)
    unnamed x6, waiting for transfers between devices  99 us
    reduce_scatter x1, waiting for transfers between devices, scatter_terms(): mine = lax.psum_scatter(terms, 'tp', scatter_dimension=1, tiled=True)  72.8 us
    ppermute x7, waiting for transfers between devices, dense_experts(): lax.ppermute(ring[-1], 'ex', [(dev, (dev + 1) % 8) for dev in range(8)])  39.2 us
    all_gather x1, waiting for transfers between devices, gather_tokens(): blocks = lax.all_gather(residual_out, ('ex', 'tp'), axis=0, tiled=False)  36.7 us
    convert_element_type x1, other arithmetic, dense_experts(): normed = (whole_rows * inverse * norm_gain).astype(jnp.bfloat16)  23.8 us
    convert_element_type x1, local copies, waits for them, and re-layouts, dense_experts(): normed = (whole_rows * inverse * norm_gain).astype(jnp.bfloat16)  17.7 us
    unnamed x25, local copies, waits for them, and re-layouts  15.3 us
    dot_general x1, matrix products, dense_experts(): jnp.dot(normed, gate_up[0].reshape(width, 2 * hidden_here), preferred_ele...  12.8 us
  transfers between devices with their start and end apart: 12, of which 11 were waited for; matrix products, arithmetic and copies ran while one was open for 2% of the time, Pallas kernels for 0%

profile of v1, /device:TPU:0, one launch (start us, length us, event | category | flops | bytes accessed | tf_op | source)
XLA Modules:
  0.0 385.1 jit_solution(18347498518203439497)
XLA Ops:
  7.2 1.0 copy.35
  8.4 4.9 %collective-permute-start = (bf16[127,1,128]{0,2,1:T(8,128)(2,1)S(1)}, bf16[127,1,128]{0,2,1:T(8,128)(2,1)S(1)}, u32[]{:S(2)}, u32[]{:S(2)}) collective-permute-start(bf16[127,1,128]{0,2,1:T(8,128)(2,1)S(1)} %slice.24), channel_id=1, source_target_pairs={{0,4},{4,8},{8,12},{12,16},{16,20},{20,24},{24,28},{1,5},{5,9},{9,... | collective-permute-start | bytes 97544 | tf_op jit(solution)/shard_map/ppermute | solution.py:14
  13.3 0.1 fusion.21
  13.5 1.1 copy.37
  14.5 0.7 exp.19
  15.2 0.9 fusion.8
  16.2 0.8 convolution_convert_fusion.2
  17.0 2.1 convolution_convert_fusion.1
  19.2 2.5 copy.40
  21.8 29.2 %reduce-scatter.10.cloned.1.call-done = bf16[720,192]{1,0:T(8,128)(2,1)} async-done(((bf16[2880,192]{1,0:T(8,128)(2,1)}), bf16[720,192]{1,0:T(8,128)(2,1)}) %reduce-scatter.10.cloned.1.call-update) | async-done | bytes 276496
  51.0 1.1 copy.41
  52.2 0.8 add_convert_fusion
  53.1 1.5 collective-permute-start.1
  54.6 5.0 %collective-permute-done.1 = f32[192,9]{0,1:T(8,128)S(1)} collective-permute-done((f32[192,9]{0,1:T(8,128)S(1)}, f32[192,9]{0,1:T(8,128)S(1)}, u32[]{:S(2)}, u32[]{:S(2)}) %collective-permute-start.1) | collective-permute-done | bytes 6944 | tf_op jit(solution)/shard_map/ppermute | solution.py:115
  59.6 6.5 %collective-permute-done.2 = f32[192,9]{0,1:T(8,128)S(1)} collective-permute-done((f32[192,9]{0,1:T(8,128)S(1)}, f32[192,9]{0,1:T(8,128)S(1)}, u32[]{:S(2)}, u32[]{:S(2)}) %collective-permute-start.2) | collective-permute-done | bytes 6944 | tf_op jit(solution)/shard_map/ppermute | solution.py:115
  66.2 6.4 %collective-permute-done.3 = f32[192,9]{0,1:T(8,128)S(1)} collective-permute-done((f32[192,9]{0,1:T(8,128)S(1)}, f32[192,9]{0,1:T(8,128)S(1)}, u32[]{:S(2)}, u32[]{:S(2)}) %collective-permute-start.3) | collective-permute-done | bytes 6944 | tf_op jit(solution)/shard_map/ppermute | solution.py:115
  72.6 6.4 %collective-permute-done.4 = f32[192,9]{0,1:T(8,128)S(1)} collective-permute-done((f32[192,9]{0,1:T(8,128)S(1)}, f32[192,9]{0,1:T(8,128)S(1)}, u32[]{:S(2)}, u32[]{:S(2)}) %collective-permute-start.4) | collective-permute-done | bytes 6944 | tf_op jit(solution)/shard_map/ppermute | solution.py:115
  79.0 6.5 %collective-permute-done.5 = f32[192,9]{0,1:T(8,128)S(1)} collective-permute-done((f32[192,9]{0,1:T(8,128)S(1)}, f32[192,9]{0,1:T(8,128)S(1)}, u32[]{:S(2)}, u32[]{:S(2)}) %collective-permute-start.5) | collective-permute-done | bytes 6944 | tf_op jit(solution)/shard_map/ppermute | solution.py:115
  85.6 6.9 %collective-permute-done.6 = f32[192,9]{0,1:T(8,128)S(1)} collective-permute-done((f32[192,9]{0,1:T(8,128)S(1)}, f32[192,9]{0,1:T(8,128)S(1)}, u32[]{:S(2)}, u32[]{:S(2)}) %collective-permute-start.6) | collective-permute-done | bytes 6944 | tf_op jit(solution)/shard_map/ppermute | solution.py:115
  92.6 5.2 %copy.44 = bf16[360,8,2,384]{3,1,2,0:T(8,128)(2,1)} copy(bf16[360,8,2,384]{3,2,1,0:T(2,128)(2,1)} %bitcast.61) | data formatting | bytes 8847360
  97.8 1.4 collective-permute-done.7
  99.5 36.7 %all-gather.3.cloned.1.call-done = bf16[6144,720]{1,0:T(8,128)(2,1)} async-done(((bf16[192,720]{1,0:T(8,128)(2,1)}), bf16[6144,720]{1,0:T(8,128)(2,1)}) %all-gather.3.cloned.1.call-update) | async-done | bytes 8847376 | tf_op jit(solution)/shard_map/all_gather | solution.py:148
  136.2 12.6 %convert.1 = f32[8,4,192,720]{3,2,1,0:T(8,128)} convert(bf16[8,4,192,720]{3,2,1,0:T(8,128)(2,1)} %bitcast.58) | non-fusion elementwise | flops 4423680 | bytes 26542080 | tf_op jit(solution)/shard_map/convert_element_type | solution.py:110
  148.8 5.7 %multiply_reduce_fusion = f32[8,192]{1,0:T(8,128)S(1)} fusion(bf16[8,4,192,720]{3,2,1,0:T(8,128)(2,1)} %bitcast.59), kind=kLoop, calls=%fused_computation.3 | loop fusion | flops 13269504 | bytes 8853504 | tf_op jit(solution)/shard_map/reduce_sum | solution.py:111
  154.6 23.8 %fusion.2 = bf16[8,192,4,720]{3,2,1,0:T(4,128)(2,1)} fusion(f32[8,4,192,720]{3,2,1,0:T(8,128)} %convert.1, f32[4,720]{1,0:T(4,128)S(1)} %mul.69, f32[8,192]{1,0:T(8,128)S(1)} %add_rsqrt_fusion), kind=kLoop, calls=%fused_computation.5 | loop fusion | flops 13271040 | bytes 26559744 | tf_op jit(solution)/shard_map/convert_element_type | solution.py:112
  178.3 17.7 %convert_element_type.74 = bf16[1536,2880]{1,0:T(8,128)(2,1)} reshape(bf16[8,192,4,720]{3,2,1,0:T(4,128)(2,1)} %fusion.2) | data formatting | bytes 17694720 | tf_op jit(solution)/shard_map/convert_element_type | solution.py:112
  196.1 12.8 %fusion.37 = f32[1536,768]{1,0:T(8,128)} fusion(bf16[1536,2880]{1,0:T(8,128)(2,1)} %convert_element_type.74, bf16[2880,768]{1,0:T(8,128)(2,1)} %bitcast.62), kind=kOutput, calls=%fused_computation.66 | convolution fusion | flops 6794772480 | bytes 17989632 | tf_op jit(solution)/shard_map/dot_general | solution.py:123
  208.9 11.2 %convolution_add_fusion = f32[1536,768]{1,0:T(8,128)} fusion(f32[1536,768]{1,0:T(8,128)} %fusion.37, bf16[128,768]{1,0:T(8,128)(2,1)S(1)} %bitcast.63, bf16[1536,2880]{1,0:T(8,128)(2,1)} %convert_element_type.74, bf16[1,2880,128]{2,1,0:T(8,128)(2,1)S(1)} %copy-done.2, s32[128]{0:T(128)S(1)} %and_select_fusion, s32[1536]{0:T(1024)S(1)} %fusion.29), kind=kOutput, calls=%fused_computation.6 | convolution fusion | flops 1436221440 | bytes 19225088 | tf_op jit(solution)/shard_map/dot_general | solution.py:129
  220.1 11.5 %convolution_convert_fusion = bf16[1536,2880]{0,1:T(8,128)(2,1)} fusion(bf16[1,384,2880]{1,2,0:T(8,128)(2,1)} %param.25, f32[1536,768]{1,0:T(8,128)} %convolution_add_fusion, f32[1536]{0:T(1024)S(1)} %select_reduce_fusion), kind=kOutput, calls=%fused_computation.4 | convolution fusion | flops 3407118336 | bytes 15783936 | tf_op jit(solution)/shard_map/dot_general | solution.py:139
  231.7 72.8 %reduce-scatter.8.cloned.1.call-done = bf16[1536,720]{0,1:T(8,128)(2,1)} async-done(((bf16[1536,2880]{0,1:T(8,128)(2,1)}), bf16[1536,720]{0,1:T(8,128)(2,1)}) %reduce-scatter.8.cloned.1.call-update) | async-done | bytes 2211856 | tf_op jit(solution)/shard_map/reduce_scatter | solution.py:154
  304.5 4.2 %copy.42 = bf16[1536,720]{1,0:T(8,128)(2,1)} copy(bf16[1536,720]{0,1:T(8,128)(2,1)} %reduce-scatter.8.cloned.1.call-done) | data formatting | bytes 4423680
  308.8 69.7 %reduce-scatter.12.cloned.1.call-done = bf16[192,720]{1,0:T(8,128)(2,1)} async-done(((bf16[1536,720]{1,0:T(8,128)(2,1)}), bf16[192,720]{1,0:T(8,128)(2,1)}) %reduce-scatter.12.cloned.1.call-update) | async-done | bytes 276496
  (51 shorter events, 1.0 us)
Async XLA Ops:
  7.2 9.9 %copy-start = (bf16[512,2880]{0,1:T(8,128)(2,1)S(1)}, bf16[512,2880]{0,1:T(8,128)(2,1)}, u32[]{:S(2)}) copy-start(bf16[512,2880]{0,1:T(8,128)(2,1)} %param.17) | copy-start | bytes 8847364
  7.2 43.8 %reduce-scatter.10.cloned.1.call-start = ((), (), s32[]{:S(2)}) async-start(), calls=%async_computation.5 | async-start | bytes 1843200
  8.4 6.8 %collective-permute-start = (bf16[127,1,128]{0,2,1:T(8,128)(2,1)S(1)}, bf16[127,1,128]{0,2,1:T(8,128)(2,1)S(1)}, u32[]{:S(2)}, u32[]{:S(2)}) collective-permute-start(bf16[127,1,128]{0,2,1:T(8,128)(2,1)S(1)} %slice.24), channel_id=1, source_target_pairs={{0,4},{4,8},{8,12},{12,16},{16,20},{20,24},{24,28},{1,5},{5,9},{9,... | collective-permute-start | bytes 97544 | tf_op jit(solution)/shard_map/ppermute | solution.py:14
  19.1 33.0 %copy-start.3 = (bf16[192,720]{1,0:T(8,128)(2,1)S(1)}, bf16[192,720]{1,0:T(8,128)(2,1)}, u32[]{:S(2)}) copy-start(bf16[192,720]{1,0:T(8,128)(2,1)} %param.13) | copy-start | bytes 829444
  19.1 33.9 %copy-start.8 = (s32[192]{0:T(256)S(1)}, s32[192]{0:T(256)}, u32[]{:S(2)}) copy-start(s32[192]{0:T(256)} %param.21) | copy-start | bytes 2308
  19.1 33.9 %copy-start.5 = (s32[192,4]{0,1:T(4,128)S(1)}, s32[192,4]{0,1:T(4,128)}, u32[]{:S(2)}) copy-start(s32[192,4]{0,1:T(4,128)} %param.20) | copy-start | bytes 9220
  19.1 33.9 %copy-start.7 = (s32[192,4]{0,1:T(4,128)S(1)}, s32[192,4]{0,1:T(4,128)}, u32[]{:S(2)}) copy-start(s32[192,4]{0,1:T(4,128)} %param.19) | copy-start | bytes 9220
  19.2 73.3 %copy-start.6 = (f32[2880]{0:T(1024)S(1)}, f32[2880]{0:T(1024)}, u32[]{:S(2)}) copy-start(f32[2880]{0:T(1024)} %param.18) | copy-start | bytes 34564
  21.7 114.5 %all-gather.3.cloned.1.call-start = ((), (), s32[]{:S(2)}) async-start(), calls=%async_computation.4 | async-start | bytes 9732096 | tf_op jit(solution)/shard_map/all_gather | solution.py:148
  53.0 251.6 %reduce-scatter.8.cloned.1.call-start = ((), (), s32[]{:S(2)}) async-start(), calls=%async_computation.3 | async-start | bytes 11059200 | tf_op jit(solution)/shard_map/reduce_scatter | solution.py:154
  53.1 6.5 %collective-permute-start.1 = (f32[192,9]{0,1:T(8,128)S(1)}, f32[192,9]{0,1:T(8,128)S(1)}, u32[]{:S(2)}, u32[]{:S(2)}) collective-permute-start(f32[192,9]{0,1:T(8,128)S(1)} %pad_maximum_fusion.1), channel_id=1, source_target_pairs={{0,4},{4,8},{8,12},{12,16},{16,20},{20,24},{24,28},{28,0},{1,5},{5... | collective-permute-start | bytes 20744 | tf_op jit(solution)/shard_map/ppermute | solution.py:115
  59.6 6.5 %collective-permute-start.2 = (f32[192,9]{0,1:T(8,128)S(1)}, f32[192,9]{0,1:T(8,128)S(1)}, u32[]{:S(2)}, u32[]{:S(2)}) collective-permute-start(f32[192,9]{0,1:T(8,128)S(1)} %collective-permute-done.1), channel_id=1, source_target_pairs={{0,4},{4,8},{8,12},{12,16},{16,20},{20,24},{24,28},{28,0},{1,5},{5... | collective-permute-start | bytes 20744 | tf_op jit(solution)/shard_map/ppermute | solution.py:115
  66.1 6.4 %collective-permute-start.3 = (f32[192,9]{0,1:T(8,128)S(1)}, f32[192,9]{0,1:T(8,128)S(1)}, u32[]{:S(2)}, u32[]{:S(2)}) collective-permute-start(f32[192,9]{0,1:T(8,128)S(1)} %collective-permute-done.2), channel_id=1, source_target_pairs={{0,4},{4,8},{8,12},{12,16},{16,20},{20,24},{24,28},{28,0},{1,5},{5... | collective-permute-start | bytes 20744 | tf_op jit(solution)/shard_map/ppermute | solution.py:115
  72.6 6.4 %collective-permute-start.4 = (f32[192,9]{0,1:T(8,128)S(1)}, f32[192,9]{0,1:T(8,128)S(1)}, u32[]{:S(2)}, u32[]{:S(2)}) collective-permute-start(f32[192,9]{0,1:T(8,128)S(1)} %collective-permute-done.3), channel_id=1, source_target_pairs={{0,4},{4,8},{8,12},{12,16},{16,20},{20,24},{24,28},{28,0},{1,5},{5... | collective-permute-start | bytes 20744 | tf_op jit(solution)/shard_map/ppermute | solution.py:115
  79.0 6.5 %collective-permute-start.5 = (f32[192,9]{0,1:T(8,128)S(1)}, f32[192,9]{0,1:T(8,128)S(1)}, u32[]{:S(2)}, u32[]{:S(2)}) collective-permute-start(f32[192,9]{0,1:T(8,128)S(1)} %collective-permute-done.4), channel_id=1, source_target_pairs={{0,4},{4,8},{8,12},{12,16},{16,20},{20,24},{24,28},{28,0},{1,5},{5... | collective-permute-start | bytes 20744 | tf_op jit(solution)/shard_map/ppermute | solution.py:115
  85.6 6.9 %collective-permute-start.6 = (f32[192,9]{0,1:T(8,128)S(1)}, f32[192,9]{0,1:T(8,128)S(1)}, u32[]{:S(2)}, u32[]{:S(2)}) collective-permute-start(f32[192,9]{0,1:T(8,128)S(1)} %collective-permute-done.5), channel_id=1, source_target_pairs={{0,4},{4,8},{8,12},{12,16},{16,20},{20,24},{24,28},{28,0},{1,5},{5... | collective-permute-start | bytes 20744 | tf_op jit(solution)/shard_map/ppermute | solution.py:115
  92.5 6.7 %collective-permute-start.7 = (f32[192,9]{0,1:T(8,128)S(1)}, f32[192,9]{0,1:T(8,128)S(1)}, u32[]{:S(2)}, u32[]{:S(2)}) collective-permute-start(f32[192,9]{0,1:T(8,128)S(1)} %collective-permute-done.6), channel_id=1, source_target_pairs={{0,4},{4,8},{8,12},{12,16},{16,20},{20,24},{24,28},{28,0},{1,5},{5... | collective-permute-start | bytes 20744 | tf_op jit(solution)/shard_map/ppermute | solution.py:115
  92.6 5.2 %copy-start.4 = (bf16[1,128,2,384]{3,2,1,0:T(2,128)(2,1)S(1)}, bf16[1,128,2,384]{3,2,1,0:T(2,128)(2,1)}, u32[]{:S(2)}) copy-start(bf16[1,128,2,384]{3,2,1,0:T(2,128)(2,1)} %param.24) | copy-start | bytes 589828
  196.1 12.8 %copy-start.2 = (bf16[1,2880,128]{2,1,0:T(8,128)(2,1)S(1)}, bf16[1,2880,128]{2,1,0:T(8,128)(2,1)}, u32[]{:S(2)}) copy-start(bf16[1,2880,128]{2,1,0:T(8,128)(2,1)} %param.23) | copy-start | bytes 2211844
  231.6 146.9 %copy-start.1 = (bf16[512,2880]{0,1:T(8,128)(2,1)S(1)}, bf16[512,2880]{0,1:T(8,128)(2,1)}, u32[]{:S(2)}) copy-start(bf16[512,2880]{0,1:T(8,128)(2,1)} %param.17) | copy-start | bytes 8847364
  231.6 146.9 %reduce-scatter.12.cloned.1.call-start = ((), (), s32[]{:S(2)}) async-start(), calls=%async_computation.6 | async-start | bytes 2654208
Sparse Core Ops, SparseCore 0:
  21.9 29.1 reduce-scatter.9
  54.5 81.7 all-gather.2
  231.8 72.7 reduce-scatter.7
  308.9 69.5 reduce-scatter.11
